TPU v7x, 32 devices: a whole 2x2x4 slice. The times are simulated.
32 devices in a mesh: gx: 2 (over y), gy: 4 (over x, core), gz: 4 (over z).
Axes of the slice: x: 2, y: 2, z: 4, core: 2. Of those that a mesh axis runs over, the one named last changes fastest.
Arguments:
- midpoints: float32 [3, 2, 4, 4, 1024], P(None, 'gx', 'gy', 'gz'), may hold values from 0 to 1
- line_vectors: float32 [3, 2, 4, 4, 1024], P(None, 'gx', 'gy', 'gz'), may hold values from -0.085 to 0.085
- burgers: float32 [3, 2, 4, 4, 1024], P(None, 'gx', 'gy', 'gz'), may hold values from -1.7 to 1.7
- live_mask: int32 [2, 4, 4, 1024], P('gx', 'gy', 'gz'), may hold values from 0 to 1, as said below
- pair_list: int32 [13, 2, 4, 4], P(None, 'gx', 'gy', 'gz'), may hold values 0 or 1
Outputs:
- forces: float32 [3, 2, 4, 4, 1024], P(None, 'gx', 'gy', 'gz')
Inputs may be any that keep to these rules, and one draw needn't show every extreme that they name: `live_mask`: the live slots of each cell are a prefix of its 1024 slots; every cell has at least 256 live slots, and some cell has all 1024 live.
All inputs are finite; a program needn't handle non-finite values. No bound on the sum of `pair_list` on one device may be relied on, other than what follows from the above.
Results may differ from a plain program's by a relative error of at most 0.0003.
Values sent between devices are 32-bit elements; how exact they have to be, the bound alone decides.
A program may use at most 64 MiB of HBM per device.

v0:
```python
import jax
import jax.numpy as jnp
from jax import lax
from jax.sharding import PartitionSpec as P

BLOCK = 128
CORE_WIDTH = 0.1
SPLIT_WIDTH = 2.0
HIGHEST = lax.Precision.HIGHEST
HALF_SHELL = [
    (step_x, step_y, step_z)
    for step_x in (-1, 0, 1)
    for step_y in (-1, 0, 1)
    for step_z in (-1, 0, 1)
    if (step_x, step_y, step_z) > (0, 0, 0)
]


def extended(block, sides, width):
    for axis, dim in sides:
        count = lax.axis_size(axis)
        forward = [(i, i + 1) for i in range(count - 1)]
        forward.append((count - 1, 0))
        backward = [(target, source) for source, target in forward]
        low = lax.ppermute(
            lax.slice_in_dim(block, block.shape[dim] - width, None, axis=dim), axis, forward
        )
        high = lax.ppermute(lax.slice_in_dim(block, 0, width, axis=dim), axis, backward)
        block = jnp.concatenate([low, block, high], axis=dim)
    return block


def from_behind(shard, axis, by):
    size = lax.axis_size(axis)
    return lax.ppermute(shard, axis, [(i, (i + by) % size) for i in range(size)])


def pair_terms(target_mid, target_weight, source_mid, source_weight, offset, with_back):
    coupling = jnp.dot(
        target_weight.T, source_weight, precision=HIGHEST, preferred_element_type=jnp.float32
    )
    deltas = [
        target_mid[component][:, None] - source_mid[component][None, :] - float(offset[component])
        for component in range(3)
    ]
    squared = deltas[0] * deltas[0] + deltas[1] * deltas[1] + deltas[2] * deltas[2]
    inner_inv = lax.rsqrt(squared + CORE_WIDTH * CORE_WIDTH)
    outer_inv = lax.rsqrt(squared + SPLIT_WIDTH * SPLIT_WIDTH)
    strength = coupling * (inner_inv * inner_inv * inner_inv - outer_inv * outer_inv * outer_inv)
    forward = jnp.stack([jnp.sum(strength * delta_part, axis=1) for delta_part in deltas])
    if with_back:
        backward = -jnp.stack([jnp.sum(strength * delta_part, axis=0) for delta_part in deltas])
        return (forward, backward)
    return forward


def line_weights(masked_line, burgers_rows):
    return (burgers_rows[:, None] * masked_line[None]).reshape(9, masked_line.shape[1])


def near_sums(
    target_mid,
    target_weight,
    source_mid,
    source_weight,
    offset,
    target_live,
    source_live,
    with_back,
):
    seg_count = target_mid.shape[1]
    slab = min(4 * BLOCK, seg_count)
    target_slabs = (target_live + slab - 1) // slab
    source_slabs = (source_live + slab - 1) // slab
    empty = jnp.zeros((3, seg_count), jnp.float32)

    def target_step(block_index, carried):
        start = block_index * slab
        part_mid = lax.dynamic_slice_in_dim(target_mid, start, slab, 1)
        part_weight = lax.dynamic_slice_in_dim(target_weight, start, slab, 1)

        def source_step(slab_index, inner):
            anchor = slab_index * slab
            slab_mid = lax.dynamic_slice_in_dim(source_mid, anchor, slab, 1)
            slab_weight = lax.dynamic_slice_in_dim(source_weight, anchor, slab, 1)
            if with_back:
                forward, backward = pair_terms(
                    part_mid, part_weight, slab_mid, slab_weight, offset, True
                )
                previous = lax.dynamic_slice_in_dim(inner[1], anchor, slab, 1)
                return (
                    inner[0] + forward,
                    lax.dynamic_update_slice_in_dim(inner[1], previous + backward, anchor, 1),
                )
            forward = pair_terms(part_mid, part_weight, slab_mid, slab_weight, offset, False)
            return (inner[0] + forward, inner[1])

        block_force, reactions = lax.fori_loop(
            0, source_slabs, source_step, (jnp.zeros((3, slab), jnp.float32), carried[1])
        )
        return (lax.dynamic_update_slice_in_dim(carried[0], block_force, start, 1), reactions)

    return lax.fori_loop(0, target_slabs, target_step, (empty, empty))


def cell_moments(weights, middle, cell_coords):
    offset_rows = [
        middle[component] + (cell_coords[component] % 2).astype(jnp.float32) - 1.0
        for component in range(3)
    ]
    moment_basis = (
        [jnp.ones_like(middle[0])]
        + offset_rows
        + [offset_rows[first] * offset_rows[second] for first in range(3) for second in range(3)]
    )
    return jnp.dot(
        weights, jnp.stack(moment_basis).T, precision=HIGHEST, preferred_element_type=jnp.float32
    )


def far_field(coarse_table, weights, middle, cell_coords, fine_dims, coarse_dims):
    coarse_count = coarse_dims[0] * coarse_dims[1] * coarse_dims[2]
    coarse_index = jnp.arange(coarse_count, dtype=jnp.int32)
    coarse_coords = (
        coarse_index // (coarse_dims[1] * coarse_dims[2]),
        coarse_index // coarse_dims[2] % coarse_dims[1],
        coarse_index % coarse_dims[2],
    )
    displace = []
    for component in range(3):
        cell_gap = cell_coords[component] - 2 * coarse_coords[component]
        cell_gap = (cell_gap + fine_dims[component] // 2) % fine_dims[component] - fine_dims[
            component
        ] // 2
        displace.append(cell_gap.astype(jnp.float32)[:, None] + middle[component][None, :] - 1.0)
    spread = jnp.stack(displace)
    weighted = jnp.einsum(
        "kcq,ci->qki", coarse_table.reshape(coarse_count, 9, 13), weights, precision=HIGHEST
    )
    monopole = weighted[0]
    dipole = weighted[1:4]
    quadrupole = weighted[4:13].reshape(3, 3, coarse_count, weights.shape[1])
    inv_radius = lax.rsqrt(jnp.sum(spread * spread, axis=0) + SPLIT_WIDTH * SPLIT_WIDTH)
    inv_cube = inv_radius * inv_radius * inv_radius
    inv_fifth = inv_cube * inv_radius * inv_radius
    inv_seventh = inv_fifth * inv_radius * inv_radius
    dipole_dot = jnp.sum(dipole * spread, axis=0)
    quad_dot = jnp.sum(quadrupole * spread[None], axis=1)
    quad_form = jnp.sum(spread * quad_dot, axis=0)
    quad_trace = quadrupole[0, 0] + quadrupole[1, 1] + quadrupole[2, 2]
    radial = (
        -monopole * inv_cube
        - 3.0 * dipole_dot * inv_fifth
        - 7.5 * quad_form * inv_seventh
        + 1.5 * quad_trace * inv_fifth
    )
    gradient = spread * radial[None] + dipole * inv_cube[None] + 3.0 * quad_dot * inv_fifth[None]
    return -jnp.sum(gradient, axis=1)


def on_device(midpoints, line_vectors, burgers, live_mask, pair_list):
    seg_count = midpoints.shape[4]
    middle = midpoints.reshape(3, seg_count)
    alive_mask = live_mask.reshape(seg_count).astype(jnp.float32)
    masked_line = line_vectors.reshape(3, seg_count) * alive_mask[None]
    burgers_rows = burgers.reshape(3, seg_count)
    weights = line_weights(masked_line, burgers_rows)
    pair_flags = pair_list.reshape(13).astype(jnp.float32)
    live_count = jnp.sum(live_mask)
    flag_row = jnp.pad(
        jnp.concatenate([pair_flags, live_count.astype(jnp.float32)[None]]), (0, seg_count - 14)
    )
    packed = jnp.concatenate([middle, masked_line, burgers_rows, flag_row[None]], axis=0).reshape(
        10, 1, 1, 1, seg_count
    )
    empty = jnp.zeros((3, seg_count), jnp.float32)
    plane = extended(packed, (("gy", 2), ("gz", 3)), 1)
    upper = from_behind(plane, "gx", -1)
    summed, unused_back = near_sums(
        middle, weights, middle, weights, (0, 0, 0), live_count, live_count, False
    )
    reaction_slots = {}
    for offset_index, offset in enumerate(HALF_SHELL):
        holder = upper if offset[0] == 1 else plane
        source = holder[:, 0, 1 + offset[1], 1 + offset[2]]
        source_weight = line_weights(source[3:6], source[6:9])
        source_live = source[9, 13].astype(jnp.int32)
        forward, backward = lax.cond(
            pair_flags[offset_index] > 0,
            lambda source=source, source_weight=source_weight, source_live=source_live, offset=offset: near_sums(
                middle, weights, source[0:3], source_weight, offset, live_count, source_live, True
            ),
            lambda: (empty, empty),
        )
        summed = summed + forward
        reaction_slots[offset] = backward
    sectioned = jnp.stack(
        [
            jnp.stack(
                [
                    jnp.stack(
                        [
                            reaction_slots.get((step_x, step_y, step_z), empty)
                            for step_z in (-1, 0, 1)
                        ],
                        axis=1,
                    )
                    for step_y in (-1, 0, 1)
                ],
                axis=1,
            )
            for step_x in (-1, 0, 1)
        ],
        axis=1,
    )
    arrived = from_behind(sectioned[:, 2], "gx", 1)
    flat_plane = sectioned[:, 1] + arrived
    plane_up = from_behind(flat_plane[:, 2], "gy", 1)
    plane_down = from_behind(flat_plane[:, 0], "gy", -1)
    column = flat_plane[:, 1] + plane_up + plane_down
    column_up = from_behind(column[:, 2], "gz", 1)
    column_down = from_behind(column[:, 0], "gz", -1)
    summed = summed + column[:, 1] + column_up + column_down
    cell_coords = (lax.axis_index("gx"), lax.axis_index("gy"), lax.axis_index("gz"))
    fine_dims = (lax.axis_size("gx"), lax.axis_size("gy"), lax.axis_size("gz"))
    coarse_dims = (fine_dims[0] // 2, fine_dims[1] // 2, fine_dims[2] // 2)
    coarse_count = coarse_dims[0] * coarse_dims[1] * coarse_dims[2]
    moments = cell_moments(weights, middle, cell_coords).reshape(1, 117)
    coarse_id = (
        cell_coords[0] // 2 * (coarse_dims[1] * coarse_dims[2])
        + cell_coords[1] // 2 * coarse_dims[2]
        + cell_coords[2] // 2
    )
    one_hot = (jnp.arange(coarse_count, dtype=jnp.int32) == coarse_id).astype(jnp.float32)
    coarse_table = lax.psum(one_hot[:, None] * moments, ("gx", "gy", "gz"))
    far = far_field(coarse_table, weights, middle, cell_coords, fine_dims, coarse_dims)
    result = (summed + far) * alive_mask[None]
    return result.reshape(3, 1, 1, 1, seg_count)


def solution(mesh):
    placed = (
        P(None, "gx", "gy", "gz", None),
        P(None, "gx", "gy", "gz", None),
        P(None, "gx", "gy", "gz", None),
        P("gx", "gy", "gz", None),
        P(None, "gx", "gy", "gz"),
    )
    return jax.shard_map(
        on_device,
        mesh=mesh,
        in_specs=placed,
        out_specs=P(None, "gx", "gy", "gz", None),
        check_vma=False,
    )
```

profile of v0, /device:TPU:1, one launch (start us, length us, event | category | flops | bytes accessed | tf_op | source)
XLA Modules:
  0.0 265.5 jit_solution(8251189360535266189)
XLA Ops:
  7.7 7.9 %while.599 = (s32[]{:T(128)}, f32[3,1024]{1,0:T(4,128)S(1)}, s32[]{:T(128)}, f32[9,1024]{1,0:T(8,128)S(1)}, f32[3,1024]{1,0:T(4,128)S(1)}, /*index=5*/s32[]{:T(1...) while((s32[]{:T(128)}, f32[3,1024]{1,0:T(4,128)S(1)}, ...), condition=%wide.region_7.8_spmd, body=%wide.region_1.7_spmd.sunk | while | flops 34081804 | bytes 199190 | solution.py:103
  16.3 38.6 %psum.7 = f32[4,9,13]{1,2,0:T(8,128)S(1)} all-reduce(f32[4,9,13]{1,2,0:T(8,128)S(1)} %copy.56), channel_id=1, replica_groups=mesh['gx'=2,'gy'=4,'gz'=4] {'gx','gy','gz'}, use_global_device_ids=true, to_apply=%region_164.165 | all-reduce | flops 468 | bytes 3744 | tf_op jit(solution)/shard_map/psum | solution.py:235
  76.1 11.2 %conditional.16 = (f32[3,1024]{1,0:T(4,128)}, f32[3,1,1024]{2,0,1:T(4,128)}) conditional(s32[]{:T(128)} %bitcast.265, () %tuple.632, (s32[]{:T(128)}, f32[10,1,3,1,1024]{4,1,3,2,0:T(1,128)S(1)}, f32[9,1024]{1,0:T(8,128)S(1)}, f32[3,1024]{1,0:T(4,128)S(1)}) %tuple.1456), branch_computations={%region_44.45_spmd, %region_45.56_spmd} | conditional | flops 35406380 | bytes 787566 | solution.py:188
  79.3 8.0 %while.570 = (s32[]{:T(128)}, f32[3,1024]{1,0:T(4,128)}, f32[3,1024]{1,0:T(4,128)}, s32[]{:T(128)}, f32[9,1024]{1,0:T(8,128)S(1)}, /*index=5*/f32[3,1024]{1,0:T(...) while((s32[]{:T(128)}, f32[3,1024]{1,0:T(4,128)}, ...), condition=%wide.region_55.55_spmd.clone, body=%wide.region_46.54_spmd.clone.sunk | while | flops 35406348 | bytes 361042 | solution.py:103
  87.3 8.1 %conditional.13 = (f32[3,1024]{1,0:T(4,128)}, f32[3,1,3,1024]{3,0,2,1:T(4,128)S(1)}) conditional(s32[]{:T(128)} %bitcast.259, () %tuple.626, (s32[]{:T(128)}, f32[10,1,3,1,1024]{4,1,3,2,0:T(1,128)S(1)}, f32[9,1024]{1,0:T(8,128)S(1)}, f32[3,1024]{1,0:T(4,128)S(1)}) %tuple.1457), branch_computations={%region_8.9_spmd, %region_9.20_spmd} | conditional | flops 35144236 | bytes 840814 | solution.py:188
  96.1 17.7 %conditional.14 = (f32[3,1024]{1,0:T(4,128)}, f32[3,1,1024]{2,0,1:T(4,128)}) conditional(s32[]{:T(128)} %bitcast.263, () %tuple.628, (s32[]{:T(128)}, f32[10,1,3,1,1024]{4,1,3,2,0:T(1,128)S(1)}, f32[9,1024]{1,0:T(8,128)S(1)}, f32[3,1024]{1,0:T(4,128)S(1)}) %tuple.1468), branch_computations={%region_20.21_spmd, %region_21.32_spmd} | conditional | flops 35406380 | bytes 787566 | solution.py:188
  99.2 14.6 %while.564 = (s32[]{:T(128)}, f32[3,1024]{1,0:T(4,128)}, f32[3,1024]{1,0:T(4,128)}, s32[]{:T(128)}, f32[9,1024]{1,0:T(8,128)S(1)}, /*index=5*/f32[3,1024]{1,0:T(...) while((s32[]{:T(128)}, f32[3,1024]{1,0:T(4,128)}, ...), condition=%wide.region_31.31_spmd.clone, body=%wide.region_22.30_spmd.clone.sunk | while | flops 35406348 | bytes 361042 | solution.py:103
  113.8 19.0 %conditional.25 = (f32[3,1024]{1,0:T(4,128)}, f32[3,1,1024]{2,0,1:T(4,128)}) conditional(s32[]{:T(128)} %bitcast.274, () %tuple.642, (s32[]{:T(128)}, f32[10,1,3,3,1024]{4,1,3,2,0:T(1,128)}, f32[9,1024]{1,0:T(8,128)S(1)}, f32[3,1024]{1,0:T(4,128)S(1)}) %tuple.1459), branch_computations={%region_152.153_spmd, %region_153.164_spmd} | conditional | flops 35668524 | bytes 1279086 | solution.py:188
  117.9 14.8 %while.597 = (s32[]{:T(128)}, f32[3,1024]{1,0:T(4,128)}, f32[3,1024]{1,0:T(4,128)}, s32[]{:T(128)}, f32[9,1024]{1,0:T(8,128)S(1)}, /*index=5*/f32[3,1024]{1,0:T(...) while((s32[]{:T(128)}, f32[3,1024]{1,0:T(4,128)}, ...), condition=%wide.region_163.163_spmd.clone, body=%wide.region_154.162_spmd.clone.sunk | while | flops 35668492 | bytes 361042 | solution.py:103
  118.0 6.7 %while.601 = (s32[]{:T(128)}, f32[3,512]{1,0:T(4,128)S(1)}, f32[3,1024]{1,0:T(4,128)}, s32[]{:T(128)}, f32[9,1024]{1,0:T(8,128)S(1)}, /*index=5*/f32[9,512]{1,0:...) while((s32[]{:T(128)}, f32[3,512]{1,0:T(4,128)S(1)}, ...), condition=%wide.region_162.161_spmd, body=%wide.region_155.160_spmd.sunk | while | flops 35659272 | bytes 155871 | solution.py:98
  125.4 6.7 %while.601 = (s32[]{:T(128)}, f32[3,512]{1,0:T(4,128)S(1)}, f32[3,1024]{1,0:T(4,128)}, s32[]{:T(128)}, f32[9,1024]{1,0:T(8,128)S(1)}, /*index=5*/f32[9,512]{1,0:...) while((s32[]{:T(128)}, f32[3,512]{1,0:T(4,128)S(1)}, ...), condition=%wide.region_162.161_spmd, body=%wide.region_155.160_spmd.sunk | while | flops 35659272 | bytes 155871 | solution.py:98
  132.7 18.7 %conditional.24 = (f32[3,1024]{1,0:T(4,128)}, f32[3,1,1024]{2,0,1:T(4,128)}) conditional(s32[]{:T(128)} %bitcast.273, () %tuple.641, (s32[]{:T(128)}, f32[10,1,3,3,1024]{4,1,3,2,0:T(1,128)}, f32[9,1024]{1,0:T(8,128)S(1)}, f32[3,1024]{1,0:T(4,128)S(1)}) %tuple.1460), branch_computations={%region_140.141_spmd, %region_141.152_spmd} | conditional | flops 35406380 | bytes 1279086 | solution.py:188
  136.9 14.6 %while.594 = (s32[]{:T(128)}, f32[3,1024]{1,0:T(4,128)}, f32[3,1024]{1,0:T(4,128)}, s32[]{:T(128)}, f32[9,1024]{1,0:T(8,128)S(1)}, /*index=5*/f32[3,1024]{1,0:T(...) while((s32[]{:T(128)}, f32[3,1024]{1,0:T(4,128)}, ...), condition=%wide.region_151.151_spmd.clone, body=%wide.region_142.150_spmd.clone.sunk | while | flops 35406348 | bytes 361042 | solution.py:103
  155.1 18.8 %conditional.20 = (f32[3,1024]{1,0:T(4,128)}, f32[3,1,1024]{2,0,1:T(4,128)}) conditional(s32[]{:T(128)} %bitcast.269, () %tuple.637, (s32[]{:T(128)}, f32[10,1,3,3,1024]{4,1,3,2,0:T(1,128)}, f32[9,1024]{1,0:T(8,128)S(1)}, f32[3,1024]{1,0:T(4,128)S(1)}) %tuple.1464), branch_computations={%region_92.93_spmd, %region_93.104_spmd} | conditional | flops 35406380 | bytes 1279086 | solution.py:188
  159.2 14.6 %while.582 = (s32[]{:T(128)}, f32[3,1024]{1,0:T(4,128)}, f32[3,1024]{1,0:T(4,128)}, s32[]{:T(128)}, f32[9,1024]{1,0:T(8,128)S(1)}, /*index=5*/f32[3,1024]{1,0:T(...) while((s32[]{:T(128)}, f32[3,1024]{1,0:T(4,128)}, ...), condition=%wide.region_103.103_spmd.clone, body=%wide.region_94.102_spmd.clone.sunk | while | flops 35406348 | bytes 361042 | solution.py:103
  159.3 6.7 %while.606 = (s32[]{:T(128)}, f32[3,512]{1,0:T(4,128)S(1)}, f32[3,1024]{1,0:T(4,128)}, s32[]{:T(128)}, f32[9,1024]{1,0:T(8,128)S(1)}, /*index=5*/f32[9,512]{1,0:...) while((s32[]{:T(128)}, f32[3,512]{1,0:T(4,128)S(1)}, ...), condition=%wide.region_102.101_spmd, body=%wide.region_95.100_spmd.sunk | while | flops 35397128 | bytes 155871 | solution.py:98
  166.6 6.7 %while.606 = (s32[]{:T(128)}, f32[3,512]{1,0:T(4,128)S(1)}, f32[3,1024]{1,0:T(4,128)}, s32[]{:T(128)}, f32[9,1024]{1,0:T(8,128)S(1)}, /*index=5*/f32[9,512]{1,0:...) while((s32[]{:T(128)}, f32[3,512]{1,0:T(4,128)S(1)}, ...), condition=%wide.region_102.101_spmd, body=%wide.region_95.100_spmd.sunk | while | flops 35397128 | bytes 155871 | solution.py:98
  173.9 12.2 %conditional.19 = (f32[3,1024]{1,0:T(4,128)}, f32[3,1,1024]{2,0,1:T(4,128)}) conditional(s32[]{:T(128)} %bitcast.268, () %tuple.636, (s32[]{:T(128)}, f32[10,1,3,3,1024]{4,1,3,2,0:T(1,128)}, f32[9,1024]{1,0:T(8,128)S(1)}, f32[3,1024]{1,0:T(4,128)S(1)}) %tuple.1465), branch_computations={%region_80.81_spmd, %region_81.92_spmd} | conditional | flops 35668524 | bytes 1279086 | solution.py:188
  178.0 8.1 %while.579 = (s32[]{:T(128)}, f32[3,1024]{1,0:T(4,128)}, f32[3,1024]{1,0:T(4,128)}, s32[]{:T(128)}, f32[9,1024]{1,0:T(8,128)S(1)}, /*index=5*/f32[3,1024]{1,0:T(...) while((s32[]{:T(128)}, f32[3,1024]{1,0:T(4,128)}, ...), condition=%wide.region_91.91_spmd.clone, body=%wide.region_82.90_spmd.clone.sunk | while | flops 35668492 | bytes 361042 | solution.py:103
  186.1 18.7 %conditional.18 = (f32[3,1024]{1,0:T(4,128)}, f32[3,1,1024]{2,0,1:T(4,128)}) conditional(s32[]{:T(128)} %bitcast.267, () %tuple.635, (s32[]{:T(128)}, f32[10,1,3,3,1024]{4,1,3,2,0:T(1,128)}, f32[9,1024]{1,0:T(8,128)S(1)}, f32[3,1024]{1,0:T(4,128)S(1)}) %tuple.1466), branch_computations={%region_68.69_spmd, %region_69.80_spmd} | conditional | flops 35406380 | bytes 1279086 | solution.py:188
  190.2 14.6 %while.576 = (s32[]{:T(128)}, f32[3,1024]{1,0:T(4,128)}, f32[3,1024]{1,0:T(4,128)}, s32[]{:T(128)}, f32[9,1024]{1,0:T(8,128)S(1)}, /*index=5*/f32[3,1024]{1,0:T(...) while((s32[]{:T(128)}, f32[3,1024]{1,0:T(4,128)}, ...), condition=%wide.region_79.79_spmd.clone, body=%wide.region_70.78_spmd.clone.sunk | while | flops 35406348 | bytes 361042 | solution.py:103
  204.8 12.3 %conditional.17 = (f32[3,1024]{1,0:T(4,128)}, f32[3,1,1024]{2,0,1:T(4,128)}) conditional(s32[]{:T(128)} %bitcast.266, () %tuple.633, (s32[]{:T(128)}, f32[10,1,3,3,1024]{4,1,3,2,0:T(1,128)}, f32[9,1024]{1,0:T(8,128)S(1)}, f32[3,1024]{1,0:T(4,128)S(1)}) %tuple.1467), branch_computations={%region_56.57_spmd, %region_57.68_spmd} | conditional | flops 35668524 | bytes 1279086 | solution.py:188
  209.0 8.1 %while.573 = (s32[]{:T(128)}, f32[3,1024]{1,0:T(4,128)}, f32[3,1024]{1,0:T(4,128)}, s32[]{:T(128)}, f32[9,1024]{1,0:T(8,128)S(1)}, /*index=5*/f32[3,1024]{1,0:T(...) while((s32[]{:T(128)}, f32[3,1024]{1,0:T(4,128)}, ...), condition=%wide.region_67.67_spmd.clone, body=%wide.region_58.66_spmd.clone.sunk | while | flops 35668492 | bytes 361042 | solution.py:103
  231.8 31.5 %collective-permute-done.9 = f32[3,1024]{1,0:T(4,128)S(1)} collective-permute-done((f32[3,1024]{1,0:T(4,128)S(1)}, f32[3,1024]{1,0:T(4,128)S(1)}, u32[]{:S(2)}, u32[]{:S(2)}) %collective-permute-start.9) | collective-permute-done | bytes 12320 | tf_op jit(solution)/shard_map/ppermute | solution.py:35
  (445 shorter events, 254.7 us)
Async XLA Ops:
  3.6 51.8 %collective-permute-start.1 = (f32[10,1,1,1,1024]{4,1,3,2,0:T(1,128)S(1)}, f32[10,1,1,1,1024]{4,1,3,2,0:T(1,128)S(1)}, u32[]{:S(2)}, u32[]{:S(2)}) collective-permute-start(f32[10,1,1,1,1024]{4,1,3,2,0:T(1,128)S(1)} %reshape.936), channel_id=1, source_target_pairs={{4,0},{8,4},{12,8},{0,12},{5,1},{9,5},{13,9},{1,13},{6,2},{10,6},{... | collective-permute-start | bytes 122888 | tf_op jit(solution)/shard_map/ppermute | solution.py:28
  3.7 51.7 %collective-permute-start = (f32[10,1,1,1,1024]{4,1,3,2,0:T(1,128)S(1)}, f32[10,1,1,1,1024]{4,1,3,2,0:T(1,128)S(1)}, u32[]{:S(2)}, u32[]{:S(2)}) collective-permute-start(f32[10,1,1,1,1024]{4,1,3,2,0:T(1,128)S(1)} %reshape.936), channel_id=1, source_target_pairs={{0,4},{4,8},{8,12},{12,0},{1,5},{5,9},{9,13},{13,1},{2,6},{6,10},{... | collective-permute-start | bytes 122888 | tf_op jit(solution)/shard_map/ppermute | solution.py:25
  55.3 18.9 %copy-start.7 = (f32[1,4,1024]{2,1,0:T(4,128)}, f32[1,4,1024]{2,1,0:T(4,128)S(1)}, u32[]{:S(2)}) copy-start(f32[1,4,1024]{2,1,0:T(4,128)S(1)} %get-tuple-element.5525) | copy-start | bytes 49156
  55.3 18.9 %copy-start.9 = (f32[1,4,1024]{2,1,0:T(4,128)}, f32[1,4,1024]{2,1,0:T(4,128)S(1)}, u32[]{:S(2)}) copy-start(f32[1,4,1024]{2,1,0:T(4,128)S(1)} %get-tuple-element.5526) | copy-start | bytes 49156
  55.4 18.8 %copy-start.5 = (f32[1,4,1024]{2,1,0:T(4,128)}, f32[1,4,1024]{2,1,0:T(4,128)S(1)}, u32[]{:S(2)}) copy-start(f32[1,4,1024]{2,1,0:T(4,128)S(1)} %add_add_fusion.2) | copy-start | bytes 49156
  55.5 5.7 %collective-permute-start.3 = (f32[10,1,3,1,1024]{4,1,3,2,0:T(1,128)S(1)}, f32[10,1,3,1,1024]{4,1,3,2,0:T(1,128)S(1)}, u32[]{:S(2)}, u32[]{:S(2)}) collective-permute-start(f32[10,1,3,1,1024]{4,1,3,2,0:T(1,128)S(1)} %constant_dynamic-update-slice_fusion.14), channel_id=1, source_target_pairs={{0,1},{1,2},{2,3},{3,0},{4,5},{5,6},{6,7},{7,4},{8,9},{9,10},{10,1... | collective-permute-start | bytes 368648 | tf_op jit(solution)/shard_map/ppermute | solution.py:25
  56.7 6.4 %collective-permute-start.2 = (f32[10,1,3,1,1024]{4,1,3,2,0:T(1,128)S(1)}, f32[10,1,3,1,1024]{4,1,3,2,0:T(1,128)S(1)}, u32[]{:S(2)}, u32[]{:S(2)}) collective-permute-start(f32[10,1,3,1,1024]{4,1,3,2,0:T(1,128)S(1)} %constant_dynamic-update-slice_fusion.14), channel_id=1, source_target_pairs={{1,0},{2,1},{3,2},{0,3},{5,4},{6,5},{7,6},{4,7},{9,8},{10,9},{11,1... | collective-permute-start | bytes 368648 | tf_op jit(solution)/shard_map/ppermute | solution.py:28
  58.9 15.3 %copy-start = (f32[1024,4,13]{0,1,2:T(4,128)}, f32[1024,4,13]{0,1,2:T(4,128)S(1)}, u32[]{:S(2)}) copy-start(f32[1024,4,13]{0,1,2:T(4,128)S(1)} %copy.69) | copy-start | bytes 638980
  59.0 15.2 %copy-start.3 = (f32[3,4,1024]{2,1,0:T(4,128)}, f32[3,4,1024]{2,1,0:T(4,128)S(1)}, u32[]{:S(2)}) copy-start(f32[3,4,1024]{2,1,0:T(4,128)S(1)} %multiply_reduce_fusion) | copy-start | bytes 147460
  64.2 49.6 %collective-permute-start.4 = (f32[10,1,3,3,1024]{4,1,3,2,0:T(1,128)}, f32[10,1,3,3,1024]{4,1,3,2,0:T(1,128)}, u32[]{:S(2)}, u32[]{:S(2)}) collective-permute-start(f32[10,1,3,3,1024]{4,1,3,2,0:T(1,128)} %pad_maximum_fusion), channel_id=1, source_target_pairs={{0,16},{16,0},{1,17},{17,1},{2,18},{18,2},{3,19},{19,3},{4,20},{20... | collective-permute-start | bytes 1105928 | tf_op jit(solution)/shard_map/ppermute | solution.py:35
  87.3 8.1 %copy-start.2 = (f32[10,1,3,1,1024]{4,1,3,2,0:T(1,128)S(1)}, f32[10,1,3,1,1024]{4,1,3,2,0:T(1,128)}, u32[]{:S(2)}) copy-start(f32[10,1,3,1,1024]{4,1,3,2,0:T(1,128)} %copy-done.1) | copy-start | bytes 368644
  219.5 4.1 %collective-permute-start.5 = (f32[3,3,3,1024]{3,0,2,1:T(4,128)S(1)}, f32[3,3,3,1024]{3,0,2,1:T(4,128)S(1)}, u32[]{:S(2)}, u32[]{:S(2)}) collective-permute-start(f32[3,3,3,1024]{3,0,2,1:T(4,128)S(1)} %pad_maximum_fusion.1), channel_id=1, source_target_pairs={{0,16},{16,0},{1,17},{17,1},{2,18},{18,2},{3,19},{19,3},{4,20},{20... | collective-permute-start | bytes 331784 | tf_op jit(solution)/shard_map/ppermute | solution.py:35
  219.6 4.0 %copy-start.12 = (f32[3,1,3,1024]{3,0,2,1:T(4,128)S(1)}, f32[3,1,3,1024]{3,0,2,1:T(4,128)}, u32[]{:S(2)}) copy-start(f32[3,1,3,1024]{3,0,2,1:T(4,128)} %copy-done.11) | copy-start | bytes 110596
  220.3 3.2 %copy-start.23 = (f32[3]{0:T(128)S(1)}, f32[3]{0:T(128)}, u32[]{:S(2)}) copy-start(f32[3]{0:T(128)} %pad.105.clone) | copy-start | bytes 40
  223.7 1.3 collective-permute-start.6
  223.7 3.6 %collective-permute-start.7 = (f32[3,3,1024]{2,0,1:T(4,128)S(1)}, f32[3,3,1024]{2,0,1:T(4,128)S(1)}, u32[]{:S(2)}, u32[]{:S(2)}) collective-permute-start(f32[3,3,1024]{2,0,1:T(4,128)S(1)} %get-tuple-element.5493), channel_id=1, source_target_pairs={{0,12},{4,0},{8,4},{12,8},{1,13},{5,1},{9,5},{13,9},{2,14},{6,2},{... | collective-permute-start | bytes 110600 | tf_op jit(solution)/shard_map/ppermute | solution.py:35
  227.3 3.4 %copy-start.8 = (f32[1,4,1024]{2,1,0:T(4,128)S(1)}, f32[1,4,1024]{2,1,0:T(4,128)}, u32[]{:S(2)}) copy-start(f32[1,4,1024]{2,1,0:T(4,128)} %copy-done.7) | copy-start | bytes 49156
  227.3 3.4 %copy-start.10 = (f32[1,4,1024]{2,1,0:T(4,128)S(1)}, f32[1,4,1024]{2,1,0:T(4,128)}, u32[]{:S(2)}) copy-start(f32[1,4,1024]{2,1,0:T(4,128)} %copy-done.9) | copy-start | bytes 49156
  227.3 3.4 %copy-start.18 = (f32[4,1024]{1,0:T(4,128)S(1)}, f32[4,1024]{1,0:T(4,128)}, u32[]{:S(2)}) copy-start(f32[4,1024]{1,0:T(4,128)} %fusion.244) | copy-start | bytes 49156
  227.3 3.4 %copy-start.4 = (f32[3,4,1024]{2,1,0:T(4,128)S(1)}, f32[3,4,1024]{2,1,0:T(4,128)}, u32[]{:S(2)}) copy-start(f32[3,4,1024]{2,1,0:T(4,128)} %copy-done.3) | copy-start | bytes 147460
  227.3 3.4 %copy-start.6 = (f32[1,4,1024]{2,1,0:T(4,128)S(1)}, f32[1,4,1024]{2,1,0:T(4,128)}, u32[]{:S(2)}) copy-start(f32[1,4,1024]{2,1,0:T(4,128)} %copy-done.5) | copy-start | bytes 49156
  227.4 4.4 %collective-permute-start.8 = (f32[3,1024]{1,0:T(4,128)S(1)}, f32[3,1024]{1,0:T(4,128)S(1)}, u32[]{:S(2)}, u32[]{:S(2)}) collective-permute-start(f32[3,1024]{1,0:T(4,128)S(1)} %get-tuple-element.5494), channel_id=1, source_target_pairs={{0,1},{1,2},{2,3},{3,0},{4,5},{5,6},{6,7},{7,4},{8,9},{9,10},{10,1... | collective-permute-start | bytes 36872 | tf_op jit(solution)/shard_map/ppermute | solution.py:35
  227.4 35.8 %collective-permute-start.9 = (f32[3,1024]{1,0:T(4,128)S(1)}, f32[3,1024]{1,0:T(4,128)S(1)}, u32[]{:S(2)}, u32[]{:S(2)}) collective-permute-start(f32[3,1024]{1,0:T(4,128)S(1)} %get-tuple-element.5495), channel_id=1, source_target_pairs={{0,3},{1,0},{2,1},{3,2},{4,7},{5,4},{6,5},{7,6},{8,11},{9,8},{10,9... | collective-permute-start | bytes 36872 | tf_op jit(solution)/shard_map/ppermute | solution.py:35
  231.6 31.7 %copy-start.17 = (f32[3,1024]{1,0:T(4,128)S(1)}, f32[3,1024]{1,0:T(4,128)}, u32[]{:S(2)}) copy-start(f32[3,1024]{1,0:T(4,128)} %copy-done.16) | copy-start | bytes 36868
  (10 other events, 10.7 us)
where the time goes:
time: 269 us; the launch traced here: 266 us
  matrix products  61.3 us (23%)
  local copies, waits for them, and re-layouts  46.4 us (17%)
  other arithmetic  44 us (16%)
  waiting for transfers between devices  42 us (16%)
  blocking collectives  38.6 us (14%)
  loops' own time  12.8 us (5%)
  starting transfers between devices  10.5 us (4%)
  between operations  9.99 us (4%)
    dot_general x32, matrix products, pair_terms(): jnp.dot(target_weight.T, source_weight, precision=HIGHEST, preferred_elem...  60.7 us
    psum x1, blocking collectives, on_device(): coarse_table = lax.psum(one_hot[:, None] * moments, ('gx', 'gy', 'gz'))  38.6 us
    ppermute x6, waiting for transfers between devices, from_behind(): lax.ppermute(shard, axis, [(i, (i + by) % size) for i in range(size)])  37.8 us
    add x28, other arithmetic, source_step(): inner[0] + forward  34.3 us
    another operation x52, local copies, waits for them, and re-layouts  19.3 us
    another operation x13, loops' own time, on_device(): lax.cond(pair_flags[offset_index] > 0, lambda source=source, source_weigh...  11.6 us
    dynamic_update_slice x20, local copies, waits for them, and re-layouts, target_step(): lax.dynamic_update_slice_in_dim(carried[0], block_force, start, 1)  10.8 us
  transfers between devices with their start and end apart: 10, of which 7 were waited for; matrix products, arithmetic and copies ran while one was open for 18% of the time, Pallas kernels for 0%

commit v1 on v0

--- a/solution.py
+++ b/solution.py
@@ -232,7 +232,7 @@
         + cell_coords[2] // 2
     )
     one_hot = (jnp.arange(coarse_count, dtype=jnp.int32) == coarse_id).astype(jnp.float32)
-    coarse_table = lax.psum(one_hot[:, None] * moments, ("gx", "gy", "gz"))
+    coarse_table = jnp.sum(lax.all_gather(one_hot[:, None] * moments, ("gx", "gy", "gz")), axis=0)
     far = far_field(coarse_table, weights, middle, cell_coords, fine_dims, coarse_dims)
     result = (summed + far) * alive_mask[None]
     return result.reshape(3, 1, 1, 1, seg_count)

time: 269 us -> 289 us (1.074)
  blocking collectives: 38.6 us -> 64.1 us
  waiting for transfers between devices: 42 us -> 37.1 us
    all_gather x0 -> x1, blocking collectives: none -> 64.1 us  [on_device(): lax.all_gather(one_hot[:, None] * moments, ('gx', 'gy', 'gz'))]
    psum x1 -> x0, blocking collectives: 38.6 us -> none  [on_device(): coarse_table = lax.psum(one_hot[:, None] * moments, ('gx', 'gy', 'gz'))]
  transfers between devices with their start and end apart: 10 -> 10, of which waited for: 7 -> 6; matrix products, arithmetic and copies ran while one was open for 18% -> 16% of each run, Pallas kernels for 0% -> 0%
where the time goes in v1:
time: 289 us; the launch traced here: 285 us
  blocking collectives  64.1 us (22%)
  matrix products  61.3 us (21%)
  local copies, waits for them, and re-layouts  45.8 us (16%)
  other arithmetic  44 us (15%)
  waiting for transfers between devices  37.1 us (13%)
  loops' own time  12.8 us (4%)
  starting transfers between devices  10.3 us (4%)
  between operations  9.99 us (3%)
    all_gather x1, blocking collectives, on_device(): lax.all_gather(one_hot[:, None] * moments, ('gx', 'gy', 'gz'))  64.1 us
    dot_general x32, matrix products, pair_terms(): jnp.dot(target_weight.T, source_weight, precision=HIGHEST, preferred_elem...  60.7 us
    ppermute x6, waiting for transfers between devices, from_behind(): lax.ppermute(shard, axis, [(i, (i + by) % size) for i in range(size)])  35 us
    add x28, other arithmetic, source_step(): inner[0] + forward  34.3 us
    another operation x52, local copies, waits for them, and re-layouts  19.3 us
    another operation x13, loops' own time, on_device(): lax.cond(pair_flags[offset_index] > 0, lambda source=source, source_weigh...  11.6 us
    dynamic_update_slice x20, local copies, waits for them, and re-layouts, target_step(): lax.dynamic_update_slice_in_dim(carried[0], block_force, start, 1)  10.8 us
  transfers between devices with their start and end apart: 10, of which 6 were waited for; matrix products, arithmetic and copies ran while one was open for 16% of the time, Pallas kernels for 0%

profile of v1, /device:TPU:1, one launch (start us, length us, event | category | flops | bytes accessed | tf_op | source)
XLA Modules:
  0.0 285.4 jit_solution(14425362702693000887)
XLA Ops:
  7.7 7.9 %while.599 = (s32[]{:T(128)}, f32[3,1024]{1,0:T(4,128)S(1)}, s32[]{:T(128)}, f32[9,1024]{1,0:T(8,128)S(1)}, f32[3,1024]{1,0:T(4,128)S(1)}, /*index=5*/s32[]{:T(1...) while((s32[]{:T(128)}, f32[3,1024]{1,0:T(4,128)S(1)}, ...), condition=%wide.region_7.8_spmd, body=%wide.region_1.7_spmd.sunk | while | flops 34081804 | bytes 199190 | solution.py:103
  15.6 64.1 %all_gather.4 = f32[32,4,117]{2,1,0:T(4,128)S(1)} all-gather(f32[1,4,117]{2,1,0:T(4,128)S(1)} %broadcast_multiply_fusion.14), channel_id=1, replica_groups=mesh['gx'=2,'gy'=4,'gz'=4] {'gx','gy','gz'}, dimensions={0}, use_global_device_ids=true | all-gather | bytes 61776 | tf_op jit(solution)/shard_map/all_gather | solution.py:235
  98.5 11.2 %conditional.16 = (f32[3,1024]{1,0:T(4,128)}, f32[3,1,1024]{2,0,1:T(4,128)}) conditional(s32[]{:T(128)} %bitcast.265, () %tuple.632, (s32[]{:T(128)}, f32[10,1,3,1,1024]{4,1,3,2,0:T(1,128)S(1)}, f32[9,1024]{1,0:T(8,128)S(1)}, f32[3,1024]{1,0:T(4,128)S(1)}) %tuple.1456), branch_computations={%region_44.45_spmd, %region_45.56_spmd} | conditional | flops 35406380 | bytes 787566 | solution.py:188
  101.7 8.0 %while.570 = (s32[]{:T(128)}, f32[3,1024]{1,0:T(4,128)}, f32[3,1024]{1,0:T(4,128)}, s32[]{:T(128)}, f32[9,1024]{1,0:T(8,128)S(1)}, /*index=5*/f32[3,1024]{1,0:T(...) while((s32[]{:T(128)}, f32[3,1024]{1,0:T(4,128)}, ...), condition=%wide.region_55.55_spmd.clone, body=%wide.region_46.54_spmd.clone.sunk | while | flops 35406348 | bytes 361042 | solution.py:103
  109.7 8.1 %conditional.13 = (f32[3,1024]{1,0:T(4,128)}, f32[3,1,3,1024]{3,0,2,1:T(4,128)S(1)}) conditional(s32[]{:T(128)} %bitcast.259, () %tuple.626, (s32[]{:T(128)}, f32[10,1,3,1,1024]{4,1,3,2,0:T(1,128)S(1)}, f32[9,1024]{1,0:T(8,128)S(1)}, f32[3,1024]{1,0:T(4,128)S(1)}) %tuple.1457), branch_computations={%region_8.9_spmd, %region_9.20_spmd} | conditional | flops 35144236 | bytes 840814 | solution.py:188
  118.5 17.7 %conditional.14 = (f32[3,1024]{1,0:T(4,128)}, f32[3,1,1024]{2,0,1:T(4,128)}) conditional(s32[]{:T(128)} %bitcast.263, () %tuple.628, (s32[]{:T(128)}, f32[10,1,3,1,1024]{4,1,3,2,0:T(1,128)S(1)}, f32[9,1024]{1,0:T(8,128)S(1)}, f32[3,1024]{1,0:T(4,128)S(1)}) %tuple.1468), branch_computations={%region_20.21_spmd, %region_21.32_spmd} | conditional | flops 35406380 | bytes 787566 | solution.py:188
  121.6 14.6 %while.564 = (s32[]{:T(128)}, f32[3,1024]{1,0:T(4,128)}, f32[3,1024]{1,0:T(4,128)}, s32[]{:T(128)}, f32[9,1024]{1,0:T(8,128)S(1)}, /*index=5*/f32[3,1024]{1,0:T(...) while((s32[]{:T(128)}, f32[3,1024]{1,0:T(4,128)}, ...), condition=%wide.region_31.31_spmd.clone, body=%wide.region_22.30_spmd.clone.sunk | while | flops 35406348 | bytes 361042 | solution.py:103
  136.2 19.0 %conditional.25 = (f32[3,1024]{1,0:T(4,128)}, f32[3,1,1024]{2,0,1:T(4,128)}) conditional(s32[]{:T(128)} %bitcast.274, () %tuple.642, (s32[]{:T(128)}, f32[10,1,3,3,1024]{4,1,3,2,0:T(1,128)}, f32[9,1024]{1,0:T(8,128)S(1)}, f32[3,1024]{1,0:T(4,128)S(1)}) %tuple.1459), branch_computations={%region_152.153_spmd, %region_153.164_spmd} | conditional | flops 35668524 | bytes 1279086 | solution.py:188
  140.3 14.8 %while.597 = (s32[]{:T(128)}, f32[3,1024]{1,0:T(4,128)}, f32[3,1024]{1,0:T(4,128)}, s32[]{:T(128)}, f32[9,1024]{1,0:T(8,128)S(1)}, /*index=5*/f32[3,1024]{1,0:T(...) while((s32[]{:T(128)}, f32[3,1024]{1,0:T(4,128)}, ...), condition=%wide.region_163.163_spmd.clone, body=%wide.region_154.162_spmd.clone.sunk | while | flops 35668492 | bytes 361042 | solution.py:103
  140.4 6.7 %while.601 = (s32[]{:T(128)}, f32[3,512]{1,0:T(4,128)S(1)}, f32[3,1024]{1,0:T(4,128)}, s32[]{:T(128)}, f32[9,1024]{1,0:T(8,128)S(1)}, /*index=5*/f32[9,512]{1,0:...) while((s32[]{:T(128)}, f32[3,512]{1,0:T(4,128)S(1)}, ...), condition=%wide.region_162.161_spmd, body=%wide.region_155.160_spmd.sunk | while | flops 35659272 | bytes 155871 | solution.py:98
  147.8 6.7 %while.601 = (s32[]{:T(128)}, f32[3,512]{1,0:T(4,128)S(1)}, f32[3,1024]{1,0:T(4,128)}, s32[]{:T(128)}, f32[9,1024]{1,0:T(8,128)S(1)}, /*index=5*/f32[9,512]{1,0:...) while((s32[]{:T(128)}, f32[3,512]{1,0:T(4,128)S(1)}, ...), condition=%wide.region_162.161_spmd, body=%wide.region_155.160_spmd.sunk | while | flops 35659272 | bytes 155871 | solution.py:98
  155.2 18.7 %conditional.24 = (f32[3,1024]{1,0:T(4,128)}, f32[3,1,1024]{2,0,1:T(4,128)}) conditional(s32[]{:T(128)} %bitcast.273, () %tuple.641, (s32[]{:T(128)}, f32[10,1,3,3,1024]{4,1,3,2,0:T(1,128)}, f32[9,1024]{1,0:T(8,128)S(1)}, f32[3,1024]{1,0:T(4,128)S(1)}) %tuple.1460), branch_computations={%region_140.141_spmd, %region_141.152_spmd} | conditional | flops 35406380 | bytes 1279086 | solution.py:188
  159.3 14.6 %while.594 = (s32[]{:T(128)}, f32[3,1024]{1,0:T(4,128)}, f32[3,1024]{1,0:T(4,128)}, s32[]{:T(128)}, f32[9,1024]{1,0:T(8,128)S(1)}, /*index=5*/f32[3,1024]{1,0:T(...) while((s32[]{:T(128)}, f32[3,1024]{1,0:T(4,128)}, ...), condition=%wide.region_151.151_spmd.clone, body=%wide.region_142.150_spmd.clone.sunk | while | flops 35406348 | bytes 361042 | solution.py:103
  177.5 18.8 %conditional.20 = (f32[3,1024]{1,0:T(4,128)}, f32[3,1,1024]{2,0,1:T(4,128)}) conditional(s32[]{:T(128)} %bitcast.269, () %tuple.637, (s32[]{:T(128)}, f32[10,1,3,3,1024]{4,1,3,2,0:T(1,128)}, f32[9,1024]{1,0:T(8,128)S(1)}, f32[3,1024]{1,0:T(4,128)S(1)}) %tuple.1464), branch_computations={%region_92.93_spmd, %region_93.104_spmd} | conditional | flops 35406380 | bytes 1279086 | solution.py:188
  181.6 14.6 %while.582 = (s32[]{:T(128)}, f32[3,1024]{1,0:T(4,128)}, f32[3,1024]{1,0:T(4,128)}, s32[]{:T(128)}, f32[9,1024]{1,0:T(8,128)S(1)}, /*index=5*/f32[3,1024]{1,0:T(...) while((s32[]{:T(128)}, f32[3,1024]{1,0:T(4,128)}, ...), condition=%wide.region_103.103_spmd.clone, body=%wide.region_94.102_spmd.clone.sunk | while | flops 35406348 | bytes 361042 | solution.py:103
  181.7 6.7 %while.606 = (s32[]{:T(128)}, f32[3,512]{1,0:T(4,128)S(1)}, f32[3,1024]{1,0:T(4,128)}, s32[]{:T(128)}, f32[9,1024]{1,0:T(8,128)S(1)}, /*index=5*/f32[9,512]{1,0:...) while((s32[]{:T(128)}, f32[3,512]{1,0:T(4,128)S(1)}, ...), condition=%wide.region_102.101_spmd, body=%wide.region_95.100_spmd.sunk | while | flops 35397128 | bytes 155871 | solution.py:98
  189.0 6.7 %while.606 = (s32[]{:T(128)}, f32[3,512]{1,0:T(4,128)S(1)}, f32[3,1024]{1,0:T(4,128)}, s32[]{:T(128)}, f32[9,1024]{1,0:T(8,128)S(1)}, /*index=5*/f32[9,512]{1,0:...) while((s32[]{:T(128)}, f32[3,512]{1,0:T(4,128)S(1)}, ...), condition=%wide.region_102.101_spmd, body=%wide.region_95.100_spmd.sunk | while | flops 35397128 | bytes 155871 | solution.py:98
  196.3 12.2 %conditional.19 = (f32[3,1024]{1,0:T(4,128)}, f32[3,1,1024]{2,0,1:T(4,128)}) conditional(s32[]{:T(128)} %bitcast.268, () %tuple.636, (s32[]{:T(128)}, f32[10,1,3,3,1024]{4,1,3,2,0:T(1,128)}, f32[9,1024]{1,0:T(8,128)S(1)}, f32[3,1024]{1,0:T(4,128)S(1)}) %tuple.1465), branch_computations={%region_80.81_spmd, %region_81.92_spmd} | conditional | flops 35668524 | bytes 1279086 | solution.py:188
  200.4 8.1 %while.579 = (s32[]{:T(128)}, f32[3,1024]{1,0:T(4,128)}, f32[3,1024]{1,0:T(4,128)}, s32[]{:T(128)}, f32[9,1024]{1,0:T(8,128)S(1)}, /*index=5*/f32[3,1024]{1,0:T(...) while((s32[]{:T(128)}, f32[3,1024]{1,0:T(4,128)}, ...), condition=%wide.region_91.91_spmd.clone, body=%wide.region_82.90_spmd.clone.sunk | while | flops 35668492 | bytes 361042 | solution.py:103
  208.5 18.7 %conditional.18 = (f32[3,1024]{1,0:T(4,128)}, f32[3,1,1024]{2,0,1:T(4,128)}) conditional(s32[]{:T(128)} %bitcast.267, () %tuple.635, (s32[]{:T(128)}, f32[10,1,3,3,1024]{4,1,3,2,0:T(1,128)}, f32[9,1024]{1,0:T(8,128)S(1)}, f32[3,1024]{1,0:T(4,128)S(1)}) %tuple.1466), branch_computations={%region_68.69_spmd, %region_69.80_spmd} | conditional | flops 35406380 | bytes 1279086 | solution.py:188
  212.7 14.6 %while.576 = (s32[]{:T(128)}, f32[3,1024]{1,0:T(4,128)}, f32[3,1024]{1,0:T(4,128)}, s32[]{:T(128)}, f32[9,1024]{1,0:T(8,128)S(1)}, /*index=5*/f32[3,1024]{1,0:T(...) while((s32[]{:T(128)}, f32[3,1024]{1,0:T(4,128)}, ...), condition=%wide.region_79.79_spmd.clone, body=%wide.region_70.78_spmd.clone.sunk | while | flops 35406348 | bytes 361042 | solution.py:103
  227.2 12.3 %conditional.17 = (f32[3,1024]{1,0:T(4,128)}, f32[3,1,1024]{2,0,1:T(4,128)}) conditional(s32[]{:T(128)} %bitcast.266, () %tuple.633, (s32[]{:T(128)}, f32[10,1,3,3,1024]{4,1,3,2,0:T(1,128)}, f32[9,1024]{1,0:T(8,128)S(1)}, f32[3,1024]{1,0:T(4,128)S(1)}) %tuple.1467), branch_computations={%region_56.57_spmd, %region_57.68_spmd} | conditional | flops 35668524 | bytes 1279086 | solution.py:188
  231.4 8.1 %while.573 = (s32[]{:T(128)}, f32[3,1024]{1,0:T(4,128)}, f32[3,1024]{1,0:T(4,128)}, s32[]{:T(128)}, f32[9,1024]{1,0:T(8,128)S(1)}, /*index=5*/f32[3,1024]{1,0:T(...) while((s32[]{:T(128)}, f32[3,1024]{1,0:T(4,128)}, ...), condition=%wide.region_67.67_spmd.clone, body=%wide.region_58.66_spmd.clone.sunk | while | flops 35668492 | bytes 361042 | solution.py:103
  256.4 26.8 %collective-permute-done.9 = f32[3,1024]{1,0:T(4,128)S(1)} collective-permute-done((f32[3,1024]{1,0:T(4,128)S(1)}, f32[3,1024]{1,0:T(4,128)S(1)}, u32[]{:S(2)}, u32[]{:S(2)}) %collective-permute-start.9) | collective-permute-done | bytes 12320 | tf_op jit(solution)/shard_map/ppermute | solution.py:35
  (445 shorter events, 253.8 us)
Async XLA Ops:
  3.6 76.9 %collective-permute-start.1 = (f32[10,1,1,1,1024]{4,1,3,2,0:T(1,128)S(1)}, f32[10,1,1,1,1024]{4,1,3,2,0:T(1,128)S(1)}, u32[]{:S(2)}, u32[]{:S(2)}) collective-permute-start(f32[10,1,1,1,1024]{4,1,3,2,0:T(1,128)S(1)} %reshape.982), channel_id=1, source_target_pairs={{4,0},{8,4},{12,8},{0,12},{5,1},{9,5},{13,9},{1,13},{6,2},{10,6},{... | collective-permute-start | bytes 122888 | tf_op jit(solution)/shard_map/ppermute | solution.py:28
  3.7 76.8 %collective-permute-start = (f32[10,1,1,1,1024]{4,1,3,2,0:T(1,128)S(1)}, f32[10,1,1,1,1024]{4,1,3,2,0:T(1,128)S(1)}, u32[]{:S(2)}, u32[]{:S(2)}) collective-permute-start(f32[10,1,1,1,1024]{4,1,3,2,0:T(1,128)S(1)} %reshape.982), channel_id=1, source_target_pairs={{0,4},{4,8},{8,12},{12,0},{1,5},{5,9},{9,13},{13,1},{2,6},{6,10},{... | collective-permute-start | bytes 122888 | tf_op jit(solution)/shard_map/ppermute | solution.py:25
  15.6 64.2 %copy-start.16 = (f32[3,1024]{1,0:T(4,128)}, f32[3,1024]{1,0:T(4,128)S(1)}, u32[]{:S(2)}) copy-start(f32[3,1024]{1,0:T(4,128)S(1)} %get-tuple-element.4222) | copy-start | bytes 36868
  80.4 16.2 %copy-start.7 = (f32[1,4,1024]{2,1,0:T(4,128)}, f32[1,4,1024]{2,1,0:T(4,128)S(1)}, u32[]{:S(2)}) copy-start(f32[1,4,1024]{2,1,0:T(4,128)S(1)} %get-tuple-element.5525) | copy-start | bytes 49156
  80.4 16.2 %copy-start.9 = (f32[1,4,1024]{2,1,0:T(4,128)}, f32[1,4,1024]{2,1,0:T(4,128)S(1)}, u32[]{:S(2)}) copy-start(f32[1,4,1024]{2,1,0:T(4,128)S(1)} %get-tuple-element.5526) | copy-start | bytes 49156
  80.4 16.1 %copy-start.5 = (f32[1,4,1024]{2,1,0:T(4,128)}, f32[1,4,1024]{2,1,0:T(4,128)S(1)}, u32[]{:S(2)}) copy-start(f32[1,4,1024]{2,1,0:T(4,128)S(1)} %add_add_fusion.2) | copy-start | bytes 49156
  80.5 5.6 %collective-permute-start.3 = (f32[10,1,3,1,1024]{4,1,3,2,0:T(1,128)S(1)}, f32[10,1,3,1,1024]{4,1,3,2,0:T(1,128)S(1)}, u32[]{:S(2)}, u32[]{:S(2)}) collective-permute-start(f32[10,1,3,1,1024]{4,1,3,2,0:T(1,128)S(1)} %constant_dynamic-update-slice_fusion.14), channel_id=1, source_target_pairs={{0,1},{1,2},{2,3},{3,0},{4,5},{5,6},{6,7},{7,4},{8,9},{9,10},{10,1... | collective-permute-start | bytes 368648 | tf_op jit(solution)/shard_map/ppermute | solution.py:25
  80.6 5.5 %collective-permute-start.2 = (f32[10,1,3,1,1024]{4,1,3,2,0:T(1,128)S(1)}, f32[10,1,3,1,1024]{4,1,3,2,0:T(1,128)S(1)}, u32[]{:S(2)}, u32[]{:S(2)}) collective-permute-start(f32[10,1,3,1,1024]{4,1,3,2,0:T(1,128)S(1)} %constant_dynamic-update-slice_fusion.14), channel_id=1, source_target_pairs={{1,0},{2,1},{3,2},{0,3},{5,4},{6,5},{7,6},{4,7},{9,8},{10,9},{11,1... | collective-permute-start | bytes 368648 | tf_op jit(solution)/shard_map/ppermute | solution.py:28
  84.0 12.6 %copy-start = (f32[1024,4,13]{0,1,2:T(4,128)}, f32[1024,4,13]{0,1,2:T(4,128)S(1)}, u32[]{:S(2)}) copy-start(f32[1024,4,13]{0,1,2:T(4,128)S(1)} %copy.70) | copy-start | bytes 638980
  84.1 12.5 %copy-start.3 = (f32[3,4,1024]{2,1,0:T(4,128)}, f32[3,4,1024]{2,1,0:T(4,128)S(1)}, u32[]{:S(2)}) copy-start(f32[3,4,1024]{2,1,0:T(4,128)S(1)} %multiply_reduce_fusion) | copy-start | bytes 147460
  87.2 49.0 %collective-permute-start.4 = (f32[10,1,3,3,1024]{4,1,3,2,0:T(1,128)}, f32[10,1,3,3,1024]{4,1,3,2,0:T(1,128)}, u32[]{:S(2)}, u32[]{:S(2)}) collective-permute-start(f32[10,1,3,3,1024]{4,1,3,2,0:T(1,128)} %pad_maximum_fusion), channel_id=1, source_target_pairs={{0,16},{16,0},{1,17},{17,1},{2,18},{18,2},{3,19},{19,3},{4,20},{20... | collective-permute-start | bytes 1105928 | tf_op jit(solution)/shard_map/ppermute | solution.py:35
  109.7 8.1 %copy-start.2 = (f32[10,1,3,1,1024]{4,1,3,2,0:T(1,128)S(1)}, f32[10,1,3,1,1024]{4,1,3,2,0:T(1,128)}, u32[]{:S(2)}) copy-start(f32[10,1,3,1,1024]{4,1,3,2,0:T(1,128)} %copy-done.1) | copy-start | bytes 368644
  241.9 5.5 %collective-permute-start.5 = (f32[3,3,3,1024]{3,0,2,1:T(4,128)S(1)}, f32[3,3,3,1024]{3,0,2,1:T(4,128)S(1)}, u32[]{:S(2)}, u32[]{:S(2)}) collective-permute-start(f32[3,3,3,1024]{3,0,2,1:T(4,128)S(1)} %pad_maximum_fusion.1), channel_id=1, source_target_pairs={{0,16},{16,0},{1,17},{17,1},{2,18},{18,2},{3,19},{19,3},{4,20},{20... | collective-permute-start | bytes 331784 | tf_op jit(solution)/shard_map/ppermute | solution.py:35
  242.0 5.4 %copy-start.12 = (f32[3,1,3,1024]{3,0,2,1:T(4,128)S(1)}, f32[3,1,3,1024]{3,0,2,1:T(4,128)}, u32[]{:S(2)}) copy-start(f32[3,1,3,1024]{3,0,2,1:T(4,128)} %copy-done.11) | copy-start | bytes 110596
  242.7 4.6 %copy-start.23 = (f32[3]{0:T(128)S(1)}, f32[3]{0:T(128)}, u32[]{:S(2)}) copy-start(f32[3]{0:T(128)} %pad.105.clone) | copy-start | bytes 40
  247.5 1.6 collective-permute-start.6
  247.6 4.3 %collective-permute-start.7 = (f32[3,3,1024]{2,0,1:T(4,128)S(1)}, f32[3,3,1024]{2,0,1:T(4,128)S(1)}, u32[]{:S(2)}, u32[]{:S(2)}) collective-permute-start(f32[3,3,1024]{2,0,1:T(4,128)S(1)} %get-tuple-element.5493), channel_id=1, source_target_pairs={{0,12},{4,0},{8,4},{12,8},{1,13},{5,1},{9,5},{13,9},{2,14},{6,2},{... | collective-permute-start | bytes 110600 | tf_op jit(solution)/shard_map/ppermute | solution.py:35
  251.9 3.4 %copy-start.8 = (f32[1,4,1024]{2,1,0:T(4,128)S(1)}, f32[1,4,1024]{2,1,0:T(4,128)}, u32[]{:S(2)}) copy-start(f32[1,4,1024]{2,1,0:T(4,128)} %copy-done.7) | copy-start | bytes 49156
  251.9 3.4 %copy-start.10 = (f32[1,4,1024]{2,1,0:T(4,128)S(1)}, f32[1,4,1024]{2,1,0:T(4,128)}, u32[]{:S(2)}) copy-start(f32[1,4,1024]{2,1,0:T(4,128)} %copy-done.9) | copy-start | bytes 49156
  251.9 3.4 %copy-start.18 = (f32[4,1024]{1,0:T(4,128)S(1)}, f32[4,1024]{1,0:T(4,128)}, u32[]{:S(2)}) copy-start(f32[4,1024]{1,0:T(4,128)} %fusion.244) | copy-start | bytes 49156
  251.9 3.4 %copy-start.4 = (f32[3,4,1024]{2,1,0:T(4,128)S(1)}, f32[3,4,1024]{2,1,0:T(4,128)}, u32[]{:S(2)}) copy-start(f32[3,4,1024]{2,1,0:T(4,128)} %copy-done.3) | copy-start | bytes 147460
  252.0 4.4 %collective-permute-start.8 = (f32[3,1024]{1,0:T(4,128)S(1)}, f32[3,1024]{1,0:T(4,128)S(1)}, u32[]{:S(2)}, u32[]{:S(2)}) collective-permute-start(f32[3,1024]{1,0:T(4,128)S(1)} %get-tuple-element.5494), channel_id=1, source_target_pairs={{0,1},{1,2},{2,3},{3,0},{4,5},{5,6},{6,7},{7,4},{8,9},{9,10},{10,1... | collective-permute-start | bytes 36872 | tf_op jit(solution)/shard_map/ppermute | solution.py:35
  252.0 31.1 %collective-permute-start.9 = (f32[3,1024]{1,0:T(4,128)S(1)}, f32[3,1024]{1,0:T(4,128)S(1)}, u32[]{:S(2)}, u32[]{:S(2)}) collective-permute-start(f32[3,1024]{1,0:T(4,128)S(1)} %get-tuple-element.5495), channel_id=1, source_target_pairs={{0,3},{1,0},{2,1},{3,2},{4,7},{5,4},{6,5},{7,6},{8,11},{9,8},{10,9... | collective-permute-start | bytes 36872 | tf_op jit(solution)/shard_map/ppermute | solution.py:35
  256.2 27.0 %copy-start.17 = (f32[3,1024]{1,0:T(4,128)S(1)}, f32[3,1024]{1,0:T(4,128)}, u32[]{:S(2)}) copy-start(f32[3,1024]{1,0:T(4,128)} %copy-done.16) | copy-start | bytes 36868
  (10 other events, 11.7 us)
